TPU v7x, 32 devices: a whole 2x2x4 slice. The times are simulated.
32 devices in a mesh: groups: 2 (over y), cubes: 16 (over z, x, core).
Axes of the slice: x: 2, y: 2, z: 4, core: 2. Of those that a mesh axis runs over, the one named last changes fastest.
Arguments:
- query_rows: bfloat16 [4096, 2560], P(('groups', 'cubes')), parts along dimension 0, may hold values from -8 to 8
- key_rows: bfloat16 [4096, 2560], P(('groups', 'cubes')), parts along dimension 0, may hold values from -9 to 9
- value_rows: bfloat16 [4096, 2560], P(('groups', 'cubes')), parts along dimension 0, may hold values from -6 to 6
- gate_logits: bfloat16 [4096, 40], P(('groups', 'cubes')), parts along dimension 0, may hold values from -6 to 6
- selection: int32 [64, 20, 8], P('groups'), parts along dimension 0, may hold values from 0 to 31, all different within a row; in each aligned block of 40 rows (0 to 39, 40 to 79, ..., all dimensions but the last counted through in order) at most 11 rows name the same one
- cube_ids: int32 [64], P('groups'), parts along dimension 0, may hold values from 0 to 31, each once
Outputs:
- mixed: bfloat16 [4096, 2560], P(('groups', 'cubes')), parts along dimension 0
There are 2 independent parts, one for each index of `groups`. A program takes and returns all parts, laid end to end along the dimension named above; each array names one. Nothing has to cross between parts.
Inputs may be any that keep to these rules, and one draw needn't show every extreme that they name: `selection`: each row of 8 names different cubes. Among the rows of one device (its 2 stored blocks with all 20 heads) no cube is named more than 11 times, a bound that some block reaches. `cube_ids`: each cube number appears once.
All inputs are finite; a program needn't handle non-finite values.
Results may differ from a plain program's by a relative error of at most 0.0047.
Values may be sent and summed in bfloat16 or wider, within the bound.
No kernel may reach another device: no remote copies, remote signals or barrier semaphores. Data moves between devices by JAX's collectives and lax.ppermute only.
A program may use at most 128 MiB of HBM per device.

v0:
```python
import math
import jax
import jax.numpy as jnp
from jax import lax
from jax.sharding import PartitionSpec as P

CUBE = 64
NEG_START = -1e30


def block_partials(query_slots, pair_slots):
    head_size = query_slots.shape[-1]
    factor = 1.0 / math.sqrt(head_size)
    slot_keys = pair_slots[:, :, :head_size]
    slot_values = pair_slots[:, :, head_size:]
    scores = (
        jnp.einsum("sqd,skd->sqk", query_slots, slot_keys, preferred_element_type=jnp.float32)
        * factor
    )
    slot_max = jnp.max(scores, axis=2)
    weights = jnp.exp(scores - slot_max[:, :, None])
    slot_total = jnp.sum(weights, axis=2)
    numerator = jnp.einsum(
        "sqk,skd->sqd",
        weights.astype(jnp.bfloat16),
        slot_values,
        preferred_element_type=jnp.float32,
    )
    return (numerator, slot_max, slot_total)


def merge_slots(state, results, slot_group):
    numerator, running_max, totals = state
    slot_numerator, slot_max, slot_total = results
    group_count = numerator.shape[0]
    slot_count = slot_group.shape[0]
    member = slot_group[:, None] == jnp.arange(group_count, dtype=jnp.int32)[None, :]
    is_valid = slot_group >= 0
    group_max = jnp.max(jnp.where(member[:, :, None], slot_max[:, None, :], -jnp.inf), axis=0)
    new_max = jnp.maximum(running_max, group_max)
    slot_base = jnp.take(new_max, jnp.maximum(slot_group, 0), axis=0)
    slot_weight = jnp.exp(jnp.where(is_valid[:, None], slot_max - slot_base, -jnp.inf))
    onehot = member.astype(jnp.float32).T
    weighted = (slot_weight[:, :, None] * slot_numerator).reshape(slot_count, -1)
    added_numerator = jnp.dot(onehot, weighted, precision=lax.Precision.HIGHEST).reshape(
        numerator.shape
    )
    added_total = jnp.dot(onehot, slot_weight * slot_total, precision=lax.Precision.HIGHEST)
    decay_factor = jnp.exp(running_max - new_max)
    return (
        numerator * decay_factor[:, :, None] + added_numerator,
        new_max,
        totals * decay_factor + added_total,
    )


def body(query_rows, key_rows, value_rows, gate_logits, selection, cube_ids):
    device_count = lax.axis_size("cubes")
    token_count = query_rows.shape[0]
    feature_width = query_rows.shape[1]
    head_count = gate_logits.shape[1] // 2
    head_size = feature_width // head_count
    local_cubes = token_count // CUBE
    total_cubes = cube_ids.shape[0]
    picks_each = selection.shape[2]
    depth_rounds = max(2, head_count * picks_each // device_count + 1)
    request_count = local_cubes * head_count * picks_each
    factor = 1.0 / math.sqrt(head_size)
    self_index = lax.axis_index("cubes")
    pooled_keys = jnp.mean(
        key_rows.reshape(local_cubes, CUBE, feature_width), axis=1, dtype=jnp.float32
    ).astype(jnp.bfloat16)
    pooled_values = jnp.mean(
        value_rows.reshape(local_cubes, CUBE, feature_width), axis=1, dtype=jnp.float32
    ).astype(jnp.bfloat16)
    query_heads = query_rows.reshape(token_count, head_count, head_size)
    start_state = (
        jnp.zeros((head_count, token_count, head_size), jnp.float32),
        jnp.full((head_count, token_count), NEG_START, jnp.float32),
        jnp.zeros((head_count, token_count), jnp.float32),
    )
    numerator, running_max, totals = start_state
    piece_keys = lax.all_gather(pooled_keys, "cubes", axis=0, tiled=True)
    piece_values = lax.all_gather(pooled_values, "cubes", axis=0, tiled=True)
    piece_rows = piece_keys.shape[0]
    scores = (
        jnp.einsum(
            "thd,jhd->htj",
            query_heads,
            piece_keys.reshape(piece_rows, head_count, head_size),
            preferred_element_type=jnp.float32,
        )
        * factor
    )
    new_max = jnp.maximum(running_max, jnp.max(scores, axis=2))
    weights = jnp.exp(scores - new_max[:, :, None])
    added = jnp.einsum(
        "htj,jhd->htd",
        weights.astype(jnp.bfloat16),
        piece_values.reshape(piece_rows, head_count, head_size),
        preferred_element_type=jnp.float32,
    )
    numerator = added
    totals = jnp.sum(weights, axis=2)
    coarse = jnp.transpose(numerator / totals[:, :, None], (1, 0, 2))
    cube_range = jnp.arange(total_cubes, dtype=jnp.int32)
    position = jnp.sum(
        jnp.where(cube_ids[None, :] == cube_range[:, None], cube_range[None, :], 0), axis=1
    )
    targets = jnp.take(position, selection.reshape(-1)).reshape(device_count, request_count)
    request_range = jnp.arange(request_count, dtype=jnp.int32)
    request_group = request_range // picks_each
    request_head = request_group % head_count
    round_range = jnp.arange(depth_rounds, dtype=jnp.int32)
    own_targets = lax.dynamic_index_in_dim(targets, self_index, 0, keepdims=False)
    same_target = own_targets[:, None] == cube_range[None, :]
    running_count = jnp.cumsum(same_target.astype(jnp.int32), axis=0)
    own_rank = jnp.sum(jnp.where(same_target, running_count, 0), axis=1) - 1
    chosen_round = same_target[None, :, :] & (own_rank[None, :, None] == round_range[:, None, None])
    wanted_all = jnp.sum(jnp.where(chosen_round, request_group[None, :, None] + 1, 0), axis=1) - 1
    own_cubes = self_index * local_cubes + jnp.arange(local_cubes, dtype=jnp.int32)
    hit_mine = targets[:, :, None] == own_cubes[None, None, :]
    mine_rank = jnp.cumsum(hit_mine.astype(jnp.int32), axis=1) - 1
    round_hit = hit_mine[None] & (mine_rank[None] == round_range[:, None, None, None])
    incoming_all = (
        jnp.sum(jnp.where(round_hit, request_head[None, None, :, None] + 1, 0), axis=2) - 1
    )
    query_groups = (
        query_rows.reshape(local_cubes, CUBE, head_count, head_size)
        .transpose(0, 2, 1, 3)
        .reshape(local_cubes * head_count, CUBE, head_size)
    )
    pair_blocks = jnp.concatenate(
        (
            key_rows.reshape(local_cubes, CUBE, head_count, head_size),
            value_rows.reshape(local_cubes, CUBE, head_count, head_size),
        ),
        axis=3,
    )
    pair_groups = pair_blocks.transpose(0, 2, 1, 3).reshape(
        local_cubes * head_count, CUBE, 2 * head_size
    )
    base_group = head_count * jnp.arange(local_cubes, dtype=jnp.int32)

    def held_pairs(incoming):
        source = (jnp.maximum(incoming, 0) + base_group[None, :]).reshape(-1)
        picked = jnp.take(pair_groups, source, axis=0)
        return jnp.where(
            (incoming >= 0).reshape(-1)[:, None, None], picked, jnp.zeros((), jnp.bfloat16)
        )

    def asked_queries(wanted):
        picked = jnp.take(query_groups, jnp.maximum(wanted, 0), axis=0)
        return jnp.where((wanted >= 0)[:, None, None], picked, jnp.zeros((), jnp.bfloat16))

    def one_round(state, tables):
        wanted, incoming = tables
        arrived = lax.all_to_all(
            held_pairs(incoming), "cubes", split_axis=0, concat_axis=0, tiled=True
        )
        results = block_partials(asked_queries(wanted), arrived)
        return (merge_slots(state, results, wanted), None)

    group_count = local_cubes * head_count
    start_state = (
        jnp.zeros((group_count, CUBE, head_size), jnp.float32),
        jnp.full((group_count, CUBE), NEG_START, jnp.float32),
        jnp.zeros((group_count, CUBE), jnp.float32),
    )
    final_state, unused = lax.scan(one_round, start_state, (wanted_all, incoming_all))
    numerator, running_max, totals = final_state
    fine_groups = numerator / totals[:, :, None]
    fine = (
        fine_groups.reshape(local_cubes, head_count, CUBE, head_size)
        .transpose(0, 2, 1, 3)
        .reshape(token_count, head_count, head_size)
    )
    gates = jax.nn.sigmoid(gate_logits.astype(jnp.float32))
    mixed = gates[:, :head_count, None] * coarse + gates[:, head_count:, None] * fine
    return mixed.reshape(token_count, feature_width).astype(jnp.bfloat16)


def solution(mesh):
    placed = (
        P(("groups", "cubes"), None),
        P(("groups", "cubes"), None),
        P(("groups", "cubes"), None),
        P(("groups", "cubes"), None),
        P("groups", None, None),
        P("groups"),
    )
    return jax.shard_map(
        body, mesh=mesh, in_specs=placed, out_specs=P(("groups", "cubes"), None), check_vma=False
    )
```

profile of v0, /device:TPU:0, one launch (start us, length us, event | category | flops | bytes accessed | tf_op | source)
XLA Modules:
  0.0 511.7 jit_solution(15837783295440268176)
XLA Ops:
  2.8 4.5 compare_select_fusion.3
  7.2 1.5 compare_reduce_fusion.24
  9.5 15.6 %select_select_fusion.1 = s32[5120]{0:T(1024)S(1)} fusion(pred[5120]{0:T(1024)(128)(4,1)S(1)} %get-tuple-element.141, pred[5120]{0:T(1024)(128)(4,1)S(1)} %get-tuple-element.140, pred[5120]{0:T(1024)(128)(4,1)S(1)} %get-tuple-element.139, pred[5120]{0:T(1024)(128)(4,1)S(1)} %get-tuple-element.138, pred[5120]{0:T(1024)(128)(4,1)S(1)} %get-tuple-element.137, ...), kind=kLoop, calls=%fused_computation.125 | loop fusion | flops 128000 | bytes 169060 | tf_op jit(solution)/shard_map/jit(_take)/gather | solution.py:110
  25.5 1.7 reduce-window.16
  32.9 432.1 %while.16 = (s32[]{:T(128)}, f32[40,64,128]{2,0,1:T(8,128)S(1)}, f32[40,64]{1,0:T(8,128)S(1)}, f32[40,64]{1,0:T(8,128)S(1)}, s32[11,32]{1,0:T(8,128)S(1)}, /*ind...) while((s32[]{:T(128)}, f32[40,64,128]{2,0,1:T(8,128)S(1)}, ...), condition=%wide.region_16.17_spmd.clone.clone, body=%wide.region_12.16_spmd.clone.clone.sunk | while | flops 197712672 | bytes 22294940 | solution.py:170
  33.6 1.9 gather_fusion
  36.8 7.4 %all-to-all-start = ((bf16[32,64,256]{2,1,0:T(8,128)(2,1)}), bf16[32,64,256]{2,1,0:T(8,128)(2,1)S(1)}, u32[]{:S(2)}, u32[]{:S(2)}) async-start(bf16[32,64,256]{2,1,0:T(8,128)(2,1)} %select_select_fusion.3), calls=%async_computation | async-start | bytes 2097152 | tf_op jit(solution)/shard_map/while/body/eval_jaxpr/all_to_all | solution.py:158
  44.2 1.4 gather_fusion.1
  45.8 21.3 %all-to-all-done = bf16[32,64,256]{2,1,0:T(8,128)(2,1)S(1)} async-done(((bf16[32,64,256]{2,1,0:T(8,128)(2,1)}), bf16[32,64,256]{2,1,0:T(8,128)(2,1)S(1)}, u32[]{:S(2)}, u32[]{:S(2)}) %all-to-all-start) | async-done | bytes 1048608 | tf_op jit(solution)/shard_map/while/body/eval_jaxpr/all_to_all | solution.py:158
  67.1 1.5 fusion.68
  70.9 1.8 convolution_add_fusion.4
  73.5 1.9 gather_fusion
  76.6 6.8 %all-to-all-start = ((bf16[32,64,256]{2,1,0:T(8,128)(2,1)}), bf16[32,64,256]{2,1,0:T(8,128)(2,1)S(1)}, u32[]{:S(2)}, u32[]{:S(2)}) async-start(bf16[32,64,256]{2,1,0:T(8,128)(2,1)} %select_select_fusion.3), calls=%async_computation | async-start | bytes 2097152 | tf_op jit(solution)/shard_map/while/body/eval_jaxpr/all_to_all | solution.py:158
  85.0 21.3 %all-to-all-done = bf16[32,64,256]{2,1,0:T(8,128)(2,1)S(1)} async-done(((bf16[32,64,256]{2,1,0:T(8,128)(2,1)}), bf16[32,64,256]{2,1,0:T(8,128)(2,1)S(1)}, u32[]{:S(2)}, u32[]{:S(2)}) %all-to-all-start) | async-done | bytes 1048608 | tf_op jit(solution)/shard_map/while/body/eval_jaxpr/all_to_all | solution.py:158
  106.3 1.5 fusion.68
  110.1 1.8 convolution_add_fusion.4
  112.7 1.9 gather_fusion
  115.8 6.8 %all-to-all-start = ((bf16[32,64,256]{2,1,0:T(8,128)(2,1)}), bf16[32,64,256]{2,1,0:T(8,128)(2,1)S(1)}, u32[]{:S(2)}, u32[]{:S(2)}) async-start(bf16[32,64,256]{2,1,0:T(8,128)(2,1)} %select_select_fusion.3), calls=%async_computation | async-start | bytes 2097152 | tf_op jit(solution)/shard_map/while/body/eval_jaxpr/all_to_all | solution.py:158
  124.2 21.3 %all-to-all-done = bf16[32,64,256]{2,1,0:T(8,128)(2,1)S(1)} async-done(((bf16[32,64,256]{2,1,0:T(8,128)(2,1)}), bf16[32,64,256]{2,1,0:T(8,128)(2,1)S(1)}, u32[]{:S(2)}, u32[]{:S(2)}) %all-to-all-start) | async-done | bytes 1048608 | tf_op jit(solution)/shard_map/while/body/eval_jaxpr/all_to_all | solution.py:158
  145.5 1.5 fusion.68
  149.3 1.8 convolution_add_fusion.4
  151.9 1.9 gather_fusion
  155.1 6.8 %all-to-all-start = ((bf16[32,64,256]{2,1,0:T(8,128)(2,1)}), bf16[32,64,256]{2,1,0:T(8,128)(2,1)S(1)}, u32[]{:S(2)}, u32[]{:S(2)}) async-start(bf16[32,64,256]{2,1,0:T(8,128)(2,1)} %select_select_fusion.3), calls=%async_computation | async-start | bytes 2097152 | tf_op jit(solution)/shard_map/while/body/eval_jaxpr/all_to_all | solution.py:158
  163.4 21.3 %all-to-all-done = bf16[32,64,256]{2,1,0:T(8,128)(2,1)S(1)} async-done(((bf16[32,64,256]{2,1,0:T(8,128)(2,1)}), bf16[32,64,256]{2,1,0:T(8,128)(2,1)S(1)}, u32[]{:S(2)}, u32[]{:S(2)}) %all-to-all-start) | async-done | bytes 1048608 | tf_op jit(solution)/shard_map/while/body/eval_jaxpr/all_to_all | solution.py:158
  184.8 1.5 fusion.68
  188.5 1.8 convolution_add_fusion.4
  191.1 1.9 gather_fusion
  194.3 6.8 %all-to-all-start = ((bf16[32,64,256]{2,1,0:T(8,128)(2,1)}), bf16[32,64,256]{2,1,0:T(8,128)(2,1)S(1)}, u32[]{:S(2)}, u32[]{:S(2)}) async-start(bf16[32,64,256]{2,1,0:T(8,128)(2,1)} %select_select_fusion.3), calls=%async_computation | async-start | bytes 2097152 | tf_op jit(solution)/shard_map/while/body/eval_jaxpr/all_to_all | solution.py:158
  202.7 21.3 %all-to-all-done = bf16[32,64,256]{2,1,0:T(8,128)(2,1)S(1)} async-done(((bf16[32,64,256]{2,1,0:T(8,128)(2,1)}), bf16[32,64,256]{2,1,0:T(8,128)(2,1)S(1)}, u32[]{:S(2)}, u32[]{:S(2)}) %all-to-all-start) | async-done | bytes 1048608 | tf_op jit(solution)/shard_map/while/body/eval_jaxpr/all_to_all | solution.py:158
  224.0 1.5 fusion.68
  227.8 1.8 convolution_add_fusion.4
  230.4 1.9 gather_fusion
  233.5 6.8 %all-to-all-start = ((bf16[32,64,256]{2,1,0:T(8,128)(2,1)}), bf16[32,64,256]{2,1,0:T(8,128)(2,1)S(1)}, u32[]{:S(2)}, u32[]{:S(2)}) async-start(bf16[32,64,256]{2,1,0:T(8,128)(2,1)} %select_select_fusion.3), calls=%async_computation | async-start | bytes 2097152 | tf_op jit(solution)/shard_map/while/body/eval_jaxpr/all_to_all | solution.py:158
  241.9 21.3 %all-to-all-done = bf16[32,64,256]{2,1,0:T(8,128)(2,1)S(1)} async-done(((bf16[32,64,256]{2,1,0:T(8,128)(2,1)}), bf16[32,64,256]{2,1,0:T(8,128)(2,1)S(1)}, u32[]{:S(2)}, u32[]{:S(2)}) %all-to-all-start) | async-done | bytes 1048608 | tf_op jit(solution)/shard_map/while/body/eval_jaxpr/all_to_all | solution.py:158
  263.2 1.5 fusion.68
  267.0 1.8 convolution_add_fusion.4
  269.6 1.9 gather_fusion
  272.7 6.8 %all-to-all-start = ((bf16[32,64,256]{2,1,0:T(8,128)(2,1)}), bf16[32,64,256]{2,1,0:T(8,128)(2,1)S(1)}, u32[]{:S(2)}, u32[]{:S(2)}) async-start(bf16[32,64,256]{2,1,0:T(8,128)(2,1)} %select_select_fusion.3), calls=%async_computation | async-start | bytes 2097152 | tf_op jit(solution)/shard_map/while/body/eval_jaxpr/all_to_all | solution.py:158
  281.1 21.3 %all-to-all-done = bf16[32,64,256]{2,1,0:T(8,128)(2,1)S(1)} async-done(((bf16[32,64,256]{2,1,0:T(8,128)(2,1)}), bf16[32,64,256]{2,1,0:T(8,128)(2,1)S(1)}, u32[]{:S(2)}, u32[]{:S(2)}) %all-to-all-start) | async-done | bytes 1048608 | tf_op jit(solution)/shard_map/while/body/eval_jaxpr/all_to_all | solution.py:158
  302.4 1.5 fusion.68
  306.2 1.8 convolution_add_fusion.4
  308.8 1.9 gather_fusion
  312.0 6.8 %all-to-all-start = ((bf16[32,64,256]{2,1,0:T(8,128)(2,1)}), bf16[32,64,256]{2,1,0:T(8,128)(2,1)S(1)}, u32[]{:S(2)}, u32[]{:S(2)}) async-start(bf16[32,64,256]{2,1,0:T(8,128)(2,1)} %select_select_fusion.3), calls=%async_computation | async-start | bytes 2097152 | tf_op jit(solution)/shard_map/while/body/eval_jaxpr/all_to_all | solution.py:158
  320.3 21.3 %all-to-all-done = bf16[32,64,256]{2,1,0:T(8,128)(2,1)S(1)} async-done(((bf16[32,64,256]{2,1,0:T(8,128)(2,1)}), bf16[32,64,256]{2,1,0:T(8,128)(2,1)S(1)}, u32[]{:S(2)}, u32[]{:S(2)}) %all-to-all-start) | async-done | bytes 1048608 | tf_op jit(solution)/shard_map/while/body/eval_jaxpr/all_to_all | solution.py:158
  341.7 1.5 fusion.68
  345.4 1.8 convolution_add_fusion.4
  348.0 1.9 gather_fusion
  351.2 6.8 %all-to-all-start = ((bf16[32,64,256]{2,1,0:T(8,128)(2,1)}), bf16[32,64,256]{2,1,0:T(8,128)(2,1)S(1)}, u32[]{:S(2)}, u32[]{:S(2)}) async-start(bf16[32,64,256]{2,1,0:T(8,128)(2,1)} %select_select_fusion.3), calls=%async_computation | async-start | bytes 2097152 | tf_op jit(solution)/shard_map/while/body/eval_jaxpr/all_to_all | solution.py:158
  359.6 21.3 %all-to-all-done = bf16[32,64,256]{2,1,0:T(8,128)(2,1)S(1)} async-done(((bf16[32,64,256]{2,1,0:T(8,128)(2,1)}), bf16[32,64,256]{2,1,0:T(8,128)(2,1)S(1)}, u32[]{:S(2)}, u32[]{:S(2)}) %all-to-all-start) | async-done | bytes 1048608 | tf_op jit(solution)/shard_map/while/body/eval_jaxpr/all_to_all | solution.py:158
  380.9 1.5 fusion.68
  384.7 1.8 convolution_add_fusion.4
  387.3 1.9 gather_fusion
  390.4 6.8 %all-to-all-start = ((bf16[32,64,256]{2,1,0:T(8,128)(2,1)}), bf16[32,64,256]{2,1,0:T(8,128)(2,1)S(1)}, u32[]{:S(2)}, u32[]{:S(2)}) async-start(bf16[32,64,256]{2,1,0:T(8,128)(2,1)} %select_select_fusion.3), calls=%async_computation | async-start | bytes 2097152 | tf_op jit(solution)/shard_map/while/body/eval_jaxpr/all_to_all | solution.py:158
  398.8 21.3 %all-to-all-done = bf16[32,64,256]{2,1,0:T(8,128)(2,1)S(1)} async-done(((bf16[32,64,256]{2,1,0:T(8,128)(2,1)}), bf16[32,64,256]{2,1,0:T(8,128)(2,1)S(1)}, u32[]{:S(2)}, u32[]{:S(2)}) %all-to-all-start) | async-done | bytes 1048608 | tf_op jit(solution)/shard_map/while/body/eval_jaxpr/all_to_all | solution.py:158
  420.1 1.5 fusion.68
  423.9 1.8 convolution_add_fusion.4
  426.5 1.9 gather_fusion
  429.6 6.8 %all-to-all-start = ((bf16[32,64,256]{2,1,0:T(8,128)(2,1)}), bf16[32,64,256]{2,1,0:T(8,128)(2,1)S(1)}, u32[]{:S(2)}, u32[]{:S(2)}) async-start(bf16[32,64,256]{2,1,0:T(8,128)(2,1)} %select_select_fusion.3), calls=%async_computation | async-start | bytes 2097152 | tf_op jit(solution)/shard_map/while/body/eval_jaxpr/all_to_all | solution.py:158
  438.0 21.3 %all-to-all-done = bf16[32,64,256]{2,1,0:T(8,128)(2,1)S(1)} async-done(((bf16[32,64,256]{2,1,0:T(8,128)(2,1)}), bf16[32,64,256]{2,1,0:T(8,128)(2,1)S(1)}, u32[]{:S(2)}, u32[]{:S(2)}) %all-to-all-start) | async-done | bytes 1048608 | tf_op jit(solution)/shard_map/while/body/eval_jaxpr/all_to_all | solution.py:158
  459.3 1.5 fusion.68
  463.1 1.8 convolution_add_fusion.4
  465.5 1.5 copy.95
  468.2 23.1 %all-gather = bf16[16,2,2560]{2,1,0:T(2,128)(2,1)S(1)} all-gather(bf16[1,2,2560]{2,1,0:T(2,128)(2,1)S(1)} %fusion.37), channel_id=1, replica_groups=mesh['groups'=2,'cubes'=16] {'cubes'}, dimensions={0}, use_global_device_ids=true | all-gather | bytes 174080 | tf_op jit(solution)/shard_map/all_gather | solution.py:83
  492.0 18.0 %all-gather.1 = bf16[16,2,2560]{2,1,0:T(2,128)(2,1)S(1)} all-gather(bf16[1,2,2560]{2,1,0:T(2,128)(2,1)S(1)} %fusion.38), channel_id=1, replica_groups=mesh['groups'=2,'cubes'=16] {'cubes'}, dimensions={0}, use_global_device_ids=true | all-gather | bytes 174080 | tf_op jit(solution)/shard_map/all_gather | solution.py:84
  (525 shorter events, 73.3 us)
Async XLA Ops:
  2.6 27.3 %copy-start.4 = (bf16[128,2560]{1,0:T(8,128)(2,1)S(1)}, bf16[128,2560]{1,0:T(8,128)(2,1)}, u32[]{:S(2)}) copy-start(bf16[128,2560]{1,0:T(8,128)(2,1)} %param.9) | copy-start | bytes 1966084
  25.4 4.9 copy-start.6
  32.9 11.3 %copy-start = (bf16[40,64,128]{2,1,0:T(8,128)(2,1)}, bf16[40,64,128]{2,1,0:T(8,128)(2,1)S(1)}, u32[]{:S(2)}) copy-start(bf16[40,64,128]{2,1,0:T(8,128)(2,1)S(1)} %get-tuple-element.288) | copy-start | bytes 1966084 | tf_op jit(solution)/shard_map/while
  33.0 12.7 %copy-start.11 = (s32[11,32]{1,0:T(8,128)}, s32[11,32]{1,0:T(8,128)S(1)}, u32[]{:S(2)}) copy-start(s32[11,32]{1,0:T(8,128)S(1)} %get-tuple-element.287) | copy-start | bytes 4228 | tf_op jit(solution)/shard_map/while
  36.8 30.3 %all-to-all-start = ((bf16[32,64,256]{2,1,0:T(8,128)(2,1)}), bf16[32,64,256]{2,1,0:T(8,128)(2,1)S(1)}, u32[]{:S(2)}, u32[]{:S(2)}) async-start(bf16[32,64,256]{2,1,0:T(8,128)(2,1)} %select_select_fusion.3), calls=%async_computation | async-start | bytes 2097152 | tf_op jit(solution)/shard_map/while/body/eval_jaxpr/all_to_all | solution.py:158
  72.8 10.7 %copy-start = (bf16[40,64,128]{2,1,0:T(8,128)(2,1)}, bf16[40,64,128]{2,1,0:T(8,128)(2,1)S(1)}, u32[]{:S(2)}) copy-start(bf16[40,64,128]{2,1,0:T(8,128)(2,1)S(1)} %get-tuple-element.288) | copy-start | bytes 1966084 | tf_op jit(solution)/shard_map/while
  72.8 12.1 %copy-start.11 = (s32[11,32]{1,0:T(8,128)}, s32[11,32]{1,0:T(8,128)S(1)}, u32[]{:S(2)}) copy-start(s32[11,32]{1,0:T(8,128)S(1)} %get-tuple-element.287) | copy-start | bytes 4228 | tf_op jit(solution)/shard_map/while
  76.6 29.7 %all-to-all-start = ((bf16[32,64,256]{2,1,0:T(8,128)(2,1)}), bf16[32,64,256]{2,1,0:T(8,128)(2,1)S(1)}, u32[]{:S(2)}, u32[]{:S(2)}) async-start(bf16[32,64,256]{2,1,0:T(8,128)(2,1)} %select_select_fusion.3), calls=%async_computation | async-start | bytes 2097152 | tf_op jit(solution)/shard_map/while/body/eval_jaxpr/all_to_all | solution.py:158
  110.1 1.9 copy-start.1
  110.1 1.9 copy-start.10
  110.1 1.9 copy-start.12
  112.0 10.7 %copy-start = (bf16[40,64,128]{2,1,0:T(8,128)(2,1)}, bf16[40,64,128]{2,1,0:T(8,128)(2,1)S(1)}, u32[]{:S(2)}) copy-start(bf16[40,64,128]{2,1,0:T(8,128)(2,1)S(1)} %get-tuple-element.288) | copy-start | bytes 1966084 | tf_op jit(solution)/shard_map/while
  112.0 12.1 %copy-start.11 = (s32[11,32]{1,0:T(8,128)}, s32[11,32]{1,0:T(8,128)S(1)}, u32[]{:S(2)}) copy-start(s32[11,32]{1,0:T(8,128)S(1)} %get-tuple-element.287) | copy-start | bytes 4228 | tf_op jit(solution)/shard_map/while
  115.8 29.7 %all-to-all-start = ((bf16[32,64,256]{2,1,0:T(8,128)(2,1)}), bf16[32,64,256]{2,1,0:T(8,128)(2,1)S(1)}, u32[]{:S(2)}, u32[]{:S(2)}) async-start(bf16[32,64,256]{2,1,0:T(8,128)(2,1)} %select_select_fusion.3), calls=%async_computation | async-start | bytes 2097152 | tf_op jit(solution)/shard_map/while/body/eval_jaxpr/all_to_all | solution.py:158
  149.3 1.9 copy-start.1
  149.3 1.9 copy-start.10
  149.3 1.9 copy-start.12
  151.2 10.7 %copy-start = (bf16[40,64,128]{2,1,0:T(8,128)(2,1)}, bf16[40,64,128]{2,1,0:T(8,128)(2,1)S(1)}, u32[]{:S(2)}) copy-start(bf16[40,64,128]{2,1,0:T(8,128)(2,1)S(1)} %get-tuple-element.288) | copy-start | bytes 1966084 | tf_op jit(solution)/shard_map/while
  151.2 12.1 %copy-start.11 = (s32[11,32]{1,0:T(8,128)}, s32[11,32]{1,0:T(8,128)S(1)}, u32[]{:S(2)}) copy-start(s32[11,32]{1,0:T(8,128)S(1)} %get-tuple-element.287) | copy-start | bytes 4228 | tf_op jit(solution)/shard_map/while
  155.1 29.7 %all-to-all-start = ((bf16[32,64,256]{2,1,0:T(8,128)(2,1)}), bf16[32,64,256]{2,1,0:T(8,128)(2,1)S(1)}, u32[]{:S(2)}, u32[]{:S(2)}) async-start(bf16[32,64,256]{2,1,0:T(8,128)(2,1)} %select_select_fusion.3), calls=%async_computation | async-start | bytes 2097152 | tf_op jit(solution)/shard_map/while/body/eval_jaxpr/all_to_all | solution.py:158
  188.5 1.9 copy-start.1
  188.5 1.9 copy-start.10
  188.5 1.9 copy-start.12
  190.4 10.7 %copy-start = (bf16[40,64,128]{2,1,0:T(8,128)(2,1)}, bf16[40,64,128]{2,1,0:T(8,128)(2,1)S(1)}, u32[]{:S(2)}) copy-start(bf16[40,64,128]{2,1,0:T(8,128)(2,1)S(1)} %get-tuple-element.288) | copy-start | bytes 1966084 | tf_op jit(solution)/shard_map/while
  190.5 12.1 %copy-start.11 = (s32[11,32]{1,0:T(8,128)}, s32[11,32]{1,0:T(8,128)S(1)}, u32[]{:S(2)}) copy-start(s32[11,32]{1,0:T(8,128)S(1)} %get-tuple-element.287) | copy-start | bytes 4228 | tf_op jit(solution)/shard_map/while
  194.3 29.7 %all-to-all-start = ((bf16[32,64,256]{2,1,0:T(8,128)(2,1)}), bf16[32,64,256]{2,1,0:T(8,128)(2,1)S(1)}, u32[]{:S(2)}, u32[]{:S(2)}) async-start(bf16[32,64,256]{2,1,0:T(8,128)(2,1)} %select_select_fusion.3), calls=%async_computation | async-start | bytes 2097152 | tf_op jit(solution)/shard_map/while/body/eval_jaxpr/all_to_all | solution.py:158
  227.7 1.9 copy-start.1
  227.7 1.9 copy-start.10
  227.8 1.9 copy-start.12
  229.7 10.7 %copy-start = (bf16[40,64,128]{2,1,0:T(8,128)(2,1)}, bf16[40,64,128]{2,1,0:T(8,128)(2,1)S(1)}, u32[]{:S(2)}) copy-start(bf16[40,64,128]{2,1,0:T(8,128)(2,1)S(1)} %get-tuple-element.288) | copy-start | bytes 1966084 | tf_op jit(solution)/shard_map/while
  229.7 12.1 %copy-start.11 = (s32[11,32]{1,0:T(8,128)}, s32[11,32]{1,0:T(8,128)S(1)}, u32[]{:S(2)}) copy-start(s32[11,32]{1,0:T(8,128)S(1)} %get-tuple-element.287) | copy-start | bytes 4228 | tf_op jit(solution)/shard_map/while
  233.5 29.7 %all-to-all-start = ((bf16[32,64,256]{2,1,0:T(8,128)(2,1)}), bf16[32,64,256]{2,1,0:T(8,128)(2,1)S(1)}, u32[]{:S(2)}, u32[]{:S(2)}) async-start(bf16[32,64,256]{2,1,0:T(8,128)(2,1)} %select_select_fusion.3), calls=%async_computation | async-start | bytes 2097152 | tf_op jit(solution)/shard_map/while/body/eval_jaxpr/all_to_all | solution.py:158
  267.0 1.9 copy-start.1
  267.0 1.9 copy-start.10
  268.9 10.7 %copy-start = (bf16[40,64,128]{2,1,0:T(8,128)(2,1)}, bf16[40,64,128]{2,1,0:T(8,128)(2,1)S(1)}, u32[]{:S(2)}) copy-start(bf16[40,64,128]{2,1,0:T(8,128)(2,1)S(1)} %get-tuple-element.288) | copy-start | bytes 1966084 | tf_op jit(solution)/shard_map/while
  268.9 12.1 %copy-start.11 = (s32[11,32]{1,0:T(8,128)}, s32[11,32]{1,0:T(8,128)S(1)}, u32[]{:S(2)}) copy-start(s32[11,32]{1,0:T(8,128)S(1)} %get-tuple-element.287) | copy-start | bytes 4228 | tf_op jit(solution)/shard_map/while
  272.7 29.7 %all-to-all-start = ((bf16[32,64,256]{2,1,0:T(8,128)(2,1)}), bf16[32,64,256]{2,1,0:T(8,128)(2,1)S(1)}, u32[]{:S(2)}, u32[]{:S(2)}) async-start(bf16[32,64,256]{2,1,0:T(8,128)(2,1)} %select_select_fusion.3), calls=%async_computation | async-start | bytes 2097152 | tf_op jit(solution)/shard_map/while/body/eval_jaxpr/all_to_all | solution.py:158
  306.2 1.9 copy-start.1
  306.2 1.9 copy-start.10
  306.2 1.9 copy-start.12
  308.1 10.7 %copy-start = (bf16[40,64,128]{2,1,0:T(8,128)(2,1)}, bf16[40,64,128]{2,1,0:T(8,128)(2,1)S(1)}, u32[]{:S(2)}) copy-start(bf16[40,64,128]{2,1,0:T(8,128)(2,1)S(1)} %get-tuple-element.288) | copy-start | bytes 1966084 | tf_op jit(solution)/shard_map/while
  308.1 12.1 %copy-start.11 = (s32[11,32]{1,0:T(8,128)}, s32[11,32]{1,0:T(8,128)S(1)}, u32[]{:S(2)}) copy-start(s32[11,32]{1,0:T(8,128)S(1)} %get-tuple-element.287) | copy-start | bytes 4228 | tf_op jit(solution)/shard_map/while
  312.0 29.7 %all-to-all-start = ((bf16[32,64,256]{2,1,0:T(8,128)(2,1)}), bf16[32,64,256]{2,1,0:T(8,128)(2,1)S(1)}, u32[]{:S(2)}, u32[]{:S(2)}) async-start(bf16[32,64,256]{2,1,0:T(8,128)(2,1)} %select_select_fusion.3), calls=%async_computation | async-start | bytes 2097152 | tf_op jit(solution)/shard_map/while/body/eval_jaxpr/all_to_all | solution.py:158
  345.4 1.9 copy-start.1
  345.4 1.9 copy-start.10
  345.4 1.9 copy-start.12
  347.3 10.7 %copy-start = (bf16[40,64,128]{2,1,0:T(8,128)(2,1)}, bf16[40,64,128]{2,1,0:T(8,128)(2,1)S(1)}, u32[]{:S(2)}) copy-start(bf16[40,64,128]{2,1,0:T(8,128)(2,1)S(1)} %get-tuple-element.288) | copy-start | bytes 1966084 | tf_op jit(solution)/shard_map/while
  347.4 12.1 %copy-start.11 = (s32[11,32]{1,0:T(8,128)}, s32[11,32]{1,0:T(8,128)S(1)}, u32[]{:S(2)}) copy-start(s32[11,32]{1,0:T(8,128)S(1)} %get-tuple-element.287) | copy-start | bytes 4228 | tf_op jit(solution)/shard_map/while
  351.2 29.7 %all-to-all-start = ((bf16[32,64,256]{2,1,0:T(8,128)(2,1)}), bf16[32,64,256]{2,1,0:T(8,128)(2,1)S(1)}, u32[]{:S(2)}, u32[]{:S(2)}) async-start(bf16[32,64,256]{2,1,0:T(8,128)(2,1)} %select_select_fusion.3), calls=%async_computation | async-start | bytes 2097152 | tf_op jit(solution)/shard_map/while/body/eval_jaxpr/all_to_all | solution.py:158
  386.6 10.7 %copy-start = (bf16[40,64,128]{2,1,0:T(8,128)(2,1)}, bf16[40,64,128]{2,1,0:T(8,128)(2,1)S(1)}, u32[]{:S(2)}) copy-start(bf16[40,64,128]{2,1,0:T(8,128)(2,1)S(1)} %get-tuple-element.288) | copy-start | bytes 1966084 | tf_op jit(solution)/shard_map/while
  386.6 12.1 %copy-start.11 = (s32[11,32]{1,0:T(8,128)}, s32[11,32]{1,0:T(8,128)S(1)}, u32[]{:S(2)}) copy-start(s32[11,32]{1,0:T(8,128)S(1)} %get-tuple-element.287) | copy-start | bytes 4228 | tf_op jit(solution)/shard_map/while
  390.4 29.7 %all-to-all-start = ((bf16[32,64,256]{2,1,0:T(8,128)(2,1)}), bf16[32,64,256]{2,1,0:T(8,128)(2,1)S(1)}, u32[]{:S(2)}, u32[]{:S(2)}) async-start(bf16[32,64,256]{2,1,0:T(8,128)(2,1)} %select_select_fusion.3), calls=%async_computation | async-start | bytes 2097152 | tf_op jit(solution)/shard_map/while/body/eval_jaxpr/all_to_all | solution.py:158
  423.9 1.9 copy-start.1
  423.9 1.9 copy-start.10
  423.9 1.9 copy-start.12
  425.8 10.7 %copy-start = (bf16[40,64,128]{2,1,0:T(8,128)(2,1)}, bf16[40,64,128]{2,1,0:T(8,128)(2,1)S(1)}, u32[]{:S(2)}) copy-start(bf16[40,64,128]{2,1,0:T(8,128)(2,1)S(1)} %get-tuple-element.288) | copy-start | bytes 1966084 | tf_op jit(solution)/shard_map/while
  425.8 12.1 %copy-start.11 = (s32[11,32]{1,0:T(8,128)}, s32[11,32]{1,0:T(8,128)S(1)}, u32[]{:S(2)}) copy-start(s32[11,32]{1,0:T(8,128)S(1)} %get-tuple-element.287) | copy-start | bytes 4228 | tf_op jit(solution)/shard_map/while
  429.6 29.7 %all-to-all-start = ((bf16[32,64,256]{2,1,0:T(8,128)(2,1)}), bf16[32,64,256]{2,1,0:T(8,128)(2,1)S(1)}, u32[]{:S(2)}, u32[]{:S(2)}) async-start(bf16[32,64,256]{2,1,0:T(8,128)(2,1)} %select_select_fusion.3), calls=%async_computation | async-start | bytes 2097152 | tf_op jit(solution)/shard_map/while/body/eval_jaxpr/all_to_all | solution.py:158
  463.1 1.9 copy-start.1
  463.1 1.9 copy-start.10
  463.1 1.9 copy-start.12
  468.1 23.7 %copy-start.13 = (bf16[128,40]{0,1:T(8,128)(2,1)S(1)}, bf16[128,40]{0,1:T(8,128)(2,1)}, u32[]{:S(2)}) copy-start(bf16[128,40]{0,1:T(8,128)(2,1)} %param.11) | copy-start | bytes 30724
  468.1 23.8 %copy-start.7 = (bf16[128,2560]{1,0:T(8,128)(2,1)S(1)}, bf16[128,2560]{1,0:T(8,128)(2,1)}, u32[]{:S(2)}) copy-start(bf16[128,2560]{1,0:T(8,128)(2,1)} %param.10) | copy-start | bytes 1966084
  491.7 18.4 %copy-start.8 = (f32[128,20,128]{0,2,1:T(8,128)S(1)}, f32[128,20,128]{0,2,1:T(8,128)}, u32[]{:S(2)}) copy-start(f32[128,20,128]{0,2,1:T(8,128)} %copy.95) | copy-start | bytes 3932164
  (21 other events, 23.7 us)
where the time goes:
time: 514 us; the launch traced here: 512 us
  waiting for transfers between devices  235 us (46%)
  starting transfers between devices  75.3 us (15%)
  local copies, waits for them, and re-layouts  61.1 us (12%)
  matrix products  48.6 us (9%)
  other arithmetic  48.2 us (9%)
  blocking collectives  41.1 us (8%)
    all_to_all x11, waiting for transfers between devices, one_round(): lax.all_to_all(held_pairs(incoming), 'cubes', split_axis=0, concat_axis=0...  235 us
    all_to_all x11, starting transfers between devices, one_round(): lax.all_to_all(held_pairs(incoming), 'cubes', split_axis=0, concat_axis=0...  75.3 us
    all_gather x1, blocking collectives, body(): piece_keys = lax.all_gather(pooled_keys, 'cubes', axis=0, tiled=True)  23.1 us
    gather x3, other arithmetic, body(): jnp.take(position, selection.reshape(-1))  21.6 us
    gather x11, local copies, waits for them, and re-layouts, held_pairs(): picked = jnp.take(pair_groups, source, axis=0)  21.3 us
    dot_general x11, matrix products, merge_slots(): jnp.dot(onehot, weighted, precision=lax.Precision.HIGHEST)  20.3 us
    all_gather x1, blocking collectives, body(): piece_values = lax.all_gather(pooled_values, 'cubes', axis=0, tiled=True)  18 us
    dot_general x11, matrix products, block_partials(): jnp.einsum('sqd,skd->sqk', query_slots, slot_keys, preferred_element_type...  16.8 us
  transfers between devices with their start and end apart: 11, of which 11 were waited for; matrix products, arithmetic and copies ran while one was open for 3% of the time, Pallas kernels for 0%

commit v1 on v0

--- a/solution.py
+++ b/solution.py
@@ -80,8 +80,13 @@
         jnp.zeros((head_count, token_count), jnp.float32),
     )
     numerator, running_max, totals = start_state
-    piece_keys = lax.all_gather(pooled_keys, "cubes", axis=0, tiled=True)
-    piece_values = lax.all_gather(pooled_values, "cubes", axis=0, tiled=True)
+    piece_keys, piece_values = jnp.split(
+        lax.all_gather(
+            jnp.concatenate([pooled_keys, pooled_values], axis=1), "cubes", axis=0, tiled=True
+        ),
+        [pooled_keys.shape[1]],
+        axis=1,
+    )
     piece_rows = piece_keys.shape[0]
     scores = (
         jnp.einsum(

time: 514 us -> 496 us (0.965)
  blocking collectives: 41.1 us -> 23.4 us
    all_gather x2 -> x1, blocking collectives: 41.1 us -> 23.4 us  [body(): lax.all_gather(jnp.concatenate([pooled_keys, pooled_values], axis=1), 'cu...]
where the time goes in v1:
time: 496 us; the launch traced here: 494 us
  waiting for transfers between devices  235 us (47%)
  starting transfers between devices  75.3 us (15%)
  local copies, waits for them, and re-layouts  60.9 us (12%)
  matrix products  48.6 us (10%)
  other arithmetic  48.2 us (10%)
  blocking collectives  23.4 us (5%)
    all_to_all x11, waiting for transfers between devices, one_round(): lax.all_to_all(held_pairs(incoming), 'cubes', split_axis=0, concat_axis=0...  235 us
    all_to_all x11, starting transfers between devices, one_round(): lax.all_to_all(held_pairs(incoming), 'cubes', split_axis=0, concat_axis=0...  75.3 us
    all_gather x1, blocking collectives, body(): lax.all_gather(jnp.concatenate([pooled_keys, pooled_values], axis=1), 'cu...  23.4 us
    gather x3, other arithmetic, body(): jnp.take(position, selection.reshape(-1))  21.6 us
    gather x11, local copies, waits for them, and re-layouts, held_pairs(): picked = jnp.take(pair_groups, source, axis=0)  21.3 us
    dot_general x11, matrix products, merge_slots(): jnp.dot(onehot, weighted, precision=lax.Precision.HIGHEST)  20.3 us
    dot_general x11, matrix products, block_partials(): jnp.einsum('sqd,skd->sqk', query_slots, slot_keys, preferred_element_type...  16.8 us
    gather x11, local copies, waits for them, and re-layouts, asked_queries(): picked = jnp.take(query_groups, jnp.maximum(wanted, 0), axis=0)  15.6 us
  transfers between devices with their start and end apart: 11, of which 11 were waited for; matrix products, arithmetic and copies ran while one was open for 3% of the time, Pallas kernels for 0%

profile of v1, /device:TPU:0, one launch (start us, length us, event | category | flops | bytes accessed | tf_op | source)
XLA Modules:
  0.0 493.8 jit_solution(16699344577678167754)
XLA Ops:
  2.8 4.5 compare_select_fusion.3
  7.2 1.5 compare_reduce_fusion.24
  9.5 15.6 %select_select_fusion.1 = s32[5120]{0:T(1024)S(1)} fusion(pred[5120]{0:T(1024)(128)(4,1)S(1)} %get-tuple-element.141, pred[5120]{0:T(1024)(128)(4,1)S(1)} %get-tuple-element.140, pred[5120]{0:T(1024)(128)(4,1)S(1)} %get-tuple-element.139, pred[5120]{0:T(1024)(128)(4,1)S(1)} %get-tuple-element.138, pred[5120]{0:T(1024)(128)(4,1)S(1)} %get-tuple-element.137, ...), kind=kLoop, calls=%fused_computation.130 | loop fusion | flops 128000 | bytes 169060 | tf_op jit(solution)/shard_map/jit(_take)/gather | solution.py:115
  25.5 1.7 reduce-window.16
  32.9 432.1 %while.16 = (s32[]{:T(128)}, f32[40,64,128]{2,0,1:T(8,128)S(1)}, f32[40,64]{1,0:T(8,128)S(1)}, f32[40,64]{1,0:T(8,128)S(1)}, s32[11,32]{1,0:T(8,128)S(1)}, /*ind...) while((s32[]{:T(128)}, f32[40,64,128]{2,0,1:T(8,128)S(1)}, ...), condition=%wide.region_16.17_spmd.clone.clone, body=%wide.region_12.16_spmd.clone.clone.sunk | while | flops 197712672 | bytes 22294940 | solution.py:175
  33.6 1.9 gather_fusion
  36.8 7.4 %all-to-all-start = ((bf16[32,64,256]{2,1,0:T(8,128)(2,1)}), bf16[32,64,256]{2,1,0:T(8,128)(2,1)S(1)}, u32[]{:S(2)}, u32[]{:S(2)}) async-start(bf16[32,64,256]{2,1,0:T(8,128)(2,1)} %select_select_fusion.3), calls=%async_computation | async-start | bytes 2097152 | tf_op jit(solution)/shard_map/while/body/eval_jaxpr/all_to_all | solution.py:163
  44.2 1.4 gather_fusion.1
  45.8 21.3 %all-to-all-done = bf16[32,64,256]{2,1,0:T(8,128)(2,1)S(1)} async-done(((bf16[32,64,256]{2,1,0:T(8,128)(2,1)}), bf16[32,64,256]{2,1,0:T(8,128)(2,1)S(1)}, u32[]{:S(2)}, u32[]{:S(2)}) %all-to-all-start) | async-done | bytes 1048608 | tf_op jit(solution)/shard_map/while/body/eval_jaxpr/all_to_all | solution.py:163
  67.1 1.5 fusion.68
  70.9 1.8 convolution_add_fusion.4
  73.5 1.9 gather_fusion
  76.6 6.8 %all-to-all-start = ((bf16[32,64,256]{2,1,0:T(8,128)(2,1)}), bf16[32,64,256]{2,1,0:T(8,128)(2,1)S(1)}, u32[]{:S(2)}, u32[]{:S(2)}) async-start(bf16[32,64,256]{2,1,0:T(8,128)(2,1)} %select_select_fusion.3), calls=%async_computation | async-start | bytes 2097152 | tf_op jit(solution)/shard_map/while/body/eval_jaxpr/all_to_all | solution.py:163
  83.5 1.4 gather_fusion.1
  85.0 21.3 %all-to-all-done = bf16[32,64,256]{2,1,0:T(8,128)(2,1)S(1)} async-done(((bf16[32,64,256]{2,1,0:T(8,128)(2,1)}), bf16[32,64,256]{2,1,0:T(8,128)(2,1)S(1)}, u32[]{:S(2)}, u32[]{:S(2)}) %all-to-all-start) | async-done | bytes 1048608 | tf_op jit(solution)/shard_map/while/body/eval_jaxpr/all_to_all | solution.py:163
  106.3 1.5 fusion.68
  110.1 1.8 convolution_add_fusion.4
  112.7 1.9 gather_fusion
  115.8 6.8 %all-to-all-start = ((bf16[32,64,256]{2,1,0:T(8,128)(2,1)}), bf16[32,64,256]{2,1,0:T(8,128)(2,1)S(1)}, u32[]{:S(2)}, u32[]{:S(2)}) async-start(bf16[32,64,256]{2,1,0:T(8,128)(2,1)} %select_select_fusion.3), calls=%async_computation | async-start | bytes 2097152 | tf_op jit(solution)/shard_map/while/body/eval_jaxpr/all_to_all | solution.py:163
  124.2 21.3 %all-to-all-done = bf16[32,64,256]{2,1,0:T(8,128)(2,1)S(1)} async-done(((bf16[32,64,256]{2,1,0:T(8,128)(2,1)}), bf16[32,64,256]{2,1,0:T(8,128)(2,1)S(1)}, u32[]{:S(2)}, u32[]{:S(2)}) %all-to-all-start) | async-done | bytes 1048608 | tf_op jit(solution)/shard_map/while/body/eval_jaxpr/all_to_all | solution.py:163
  145.5 1.5 fusion.68
  149.3 1.8 convolution_add_fusion.4
  151.9 1.9 gather_fusion
  155.1 6.8 %all-to-all-start = ((bf16[32,64,256]{2,1,0:T(8,128)(2,1)}), bf16[32,64,256]{2,1,0:T(8,128)(2,1)S(1)}, u32[]{:S(2)}, u32[]{:S(2)}) async-start(bf16[32,64,256]{2,1,0:T(8,128)(2,1)} %select_select_fusion.3), calls=%async_computation | async-start | bytes 2097152 | tf_op jit(solution)/shard_map/while/body/eval_jaxpr/all_to_all | solution.py:163
  163.4 21.3 %all-to-all-done = bf16[32,64,256]{2,1,0:T(8,128)(2,1)S(1)} async-done(((bf16[32,64,256]{2,1,0:T(8,128)(2,1)}), bf16[32,64,256]{2,1,0:T(8,128)(2,1)S(1)}, u32[]{:S(2)}, u32[]{:S(2)}) %all-to-all-start) | async-done | bytes 1048608 | tf_op jit(solution)/shard_map/while/body/eval_jaxpr/all_to_all | solution.py:163
  184.8 1.5 fusion.68
  188.5 1.8 convolution_add_fusion.4
  191.1 1.9 gather_fusion
  194.3 6.8 %all-to-all-start = ((bf16[32,64,256]{2,1,0:T(8,128)(2,1)}), bf16[32,64,256]{2,1,0:T(8,128)(2,1)S(1)}, u32[]{:S(2)}, u32[]{:S(2)}) async-start(bf16[32,64,256]{2,1,0:T(8,128)(2,1)} %select_select_fusion.3), calls=%async_computation | async-start | bytes 2097152 | tf_op jit(solution)/shard_map/while/body/eval_jaxpr/all_to_all | solution.py:163
  202.7 21.3 %all-to-all-done = bf16[32,64,256]{2,1,0:T(8,128)(2,1)S(1)} async-done(((bf16[32,64,256]{2,1,0:T(8,128)(2,1)}), bf16[32,64,256]{2,1,0:T(8,128)(2,1)S(1)}, u32[]{:S(2)}, u32[]{:S(2)}) %all-to-all-start) | async-done | bytes 1048608 | tf_op jit(solution)/shard_map/while/body/eval_jaxpr/all_to_all | solution.py:163
  224.0 1.5 fusion.68
  227.8 1.8 convolution_add_fusion.4
  230.4 1.9 gather_fusion
  233.5 6.8 %all-to-all-start = ((bf16[32,64,256]{2,1,0:T(8,128)(2,1)}), bf16[32,64,256]{2,1,0:T(8,128)(2,1)S(1)}, u32[]{:S(2)}, u32[]{:S(2)}) async-start(bf16[32,64,256]{2,1,0:T(8,128)(2,1)} %select_select_fusion.3), calls=%async_computation | async-start | bytes 2097152 | tf_op jit(solution)/shard_map/while/body/eval_jaxpr/all_to_all | solution.py:163
  241.9 21.3 %all-to-all-done = bf16[32,64,256]{2,1,0:T(8,128)(2,1)S(1)} async-done(((bf16[32,64,256]{2,1,0:T(8,128)(2,1)}), bf16[32,64,256]{2,1,0:T(8,128)(2,1)S(1)}, u32[]{:S(2)}, u32[]{:S(2)}) %all-to-all-start) | async-done | bytes 1048608 | tf_op jit(solution)/shard_map/while/body/eval_jaxpr/all_to_all | solution.py:163
  263.2 1.5 fusion.68
  267.0 1.8 convolution_add_fusion.4
  269.6 1.9 gather_fusion
  272.7 6.8 %all-to-all-start = ((bf16[32,64,256]{2,1,0:T(8,128)(2,1)}), bf16[32,64,256]{2,1,0:T(8,128)(2,1)S(1)}, u32[]{:S(2)}, u32[]{:S(2)}) async-start(bf16[32,64,256]{2,1,0:T(8,128)(2,1)} %select_select_fusion.3), calls=%async_computation | async-start | bytes 2097152 | tf_op jit(solution)/shard_map/while/body/eval_jaxpr/all_to_all | solution.py:163
  281.1 21.3 %all-to-all-done = bf16[32,64,256]{2,1,0:T(8,128)(2,1)S(1)} async-done(((bf16[32,64,256]{2,1,0:T(8,128)(2,1)}), bf16[32,64,256]{2,1,0:T(8,128)(2,1)S(1)}, u32[]{:S(2)}, u32[]{:S(2)}) %all-to-all-start) | async-done | bytes 1048608 | tf_op jit(solution)/shard_map/while/body/eval_jaxpr/all_to_all | solution.py:163
  302.4 1.5 fusion.68
  306.2 1.8 convolution_add_fusion.4
  308.8 1.9 gather_fusion
  312.0 6.8 %all-to-all-start = ((bf16[32,64,256]{2,1,0:T(8,128)(2,1)}), bf16[32,64,256]{2,1,0:T(8,128)(2,1)S(1)}, u32[]{:S(2)}, u32[]{:S(2)}) async-start(bf16[32,64,256]{2,1,0:T(8,128)(2,1)} %select_select_fusion.3), calls=%async_computation | async-start | bytes 2097152 | tf_op jit(solution)/shard_map/while/body/eval_jaxpr/all_to_all | solution.py:163
  320.3 21.3 %all-to-all-done = bf16[32,64,256]{2,1,0:T(8,128)(2,1)S(1)} async-done(((bf16[32,64,256]{2,1,0:T(8,128)(2,1)}), bf16[32,64,256]{2,1,0:T(8,128)(2,1)S(1)}, u32[]{:S(2)}, u32[]{:S(2)}) %all-to-all-start) | async-done | bytes 1048608 | tf_op jit(solution)/shard_map/while/body/eval_jaxpr/all_to_all | solution.py:163
  341.7 1.5 fusion.68
  345.4 1.8 convolution_add_fusion.4
  348.0 1.9 gather_fusion
  351.2 6.8 %all-to-all-start = ((bf16[32,64,256]{2,1,0:T(8,128)(2,1)}), bf16[32,64,256]{2,1,0:T(8,128)(2,1)S(1)}, u32[]{:S(2)}, u32[]{:S(2)}) async-start(bf16[32,64,256]{2,1,0:T(8,128)(2,1)} %select_select_fusion.3), calls=%async_computation | async-start | bytes 2097152 | tf_op jit(solution)/shard_map/while/body/eval_jaxpr/all_to_all | solution.py:163
  359.6 21.3 %all-to-all-done = bf16[32,64,256]{2,1,0:T(8,128)(2,1)S(1)} async-done(((bf16[32,64,256]{2,1,0:T(8,128)(2,1)}), bf16[32,64,256]{2,1,0:T(8,128)(2,1)S(1)}, u32[]{:S(2)}, u32[]{:S(2)}) %all-to-all-start) | async-done | bytes 1048608 | tf_op jit(solution)/shard_map/while/body/eval_jaxpr/all_to_all | solution.py:163
  380.9 1.5 fusion.68
  384.7 1.8 convolution_add_fusion.4
  387.3 1.9 gather_fusion
  390.4 6.8 %all-to-all-start = ((bf16[32,64,256]{2,1,0:T(8,128)(2,1)}), bf16[32,64,256]{2,1,0:T(8,128)(2,1)S(1)}, u32[]{:S(2)}, u32[]{:S(2)}) async-start(bf16[32,64,256]{2,1,0:T(8,128)(2,1)} %select_select_fusion.3), calls=%async_computation | async-start | bytes 2097152 | tf_op jit(solution)/shard_map/while/body/eval_jaxpr/all_to_all | solution.py:163
  398.8 21.3 %all-to-all-done = bf16[32,64,256]{2,1,0:T(8,128)(2,1)S(1)} async-done(((bf16[32,64,256]{2,1,0:T(8,128)(2,1)}), bf16[32,64,256]{2,1,0:T(8,128)(2,1)S(1)}, u32[]{:S(2)}, u32[]{:S(2)}) %all-to-all-start) | async-done | bytes 1048608 | tf_op jit(solution)/shard_map/while/body/eval_jaxpr/all_to_all | solution.py:163
  420.1 1.5 fusion.68
  423.9 1.8 convolution_add_fusion.4
  426.5 1.9 gather_fusion
  429.6 6.8 %all-to-all-start = ((bf16[32,64,256]{2,1,0:T(8,128)(2,1)}), bf16[32,64,256]{2,1,0:T(8,128)(2,1)S(1)}, u32[]{:S(2)}, u32[]{:S(2)}) async-start(bf16[32,64,256]{2,1,0:T(8,128)(2,1)} %select_select_fusion.3), calls=%async_computation | async-start | bytes 2097152 | tf_op jit(solution)/shard_map/while/body/eval_jaxpr/all_to_all | solution.py:163
  438.0 21.3 %all-to-all-done = bf16[32,64,256]{2,1,0:T(8,128)(2,1)S(1)} async-done(((bf16[32,64,256]{2,1,0:T(8,128)(2,1)}), bf16[32,64,256]{2,1,0:T(8,128)(2,1)S(1)}, u32[]{:S(2)}, u32[]{:S(2)}) %all-to-all-start) | async-done | bytes 1048608 | tf_op jit(solution)/shard_map/while/body/eval_jaxpr/all_to_all | solution.py:163
  459.3 1.5 fusion.68
  463.1 1.8 convolution_add_fusion.4
  465.5 1.5 copy.95
  467.3 23.4 %all-gather = bf16[16,2,5120]{2,1,0:T(2,128)(2,1)S(1)} all-gather(bf16[1,2,5120]{2,1,0:T(2,128)(2,1)S(1)} %maximum_bitcast_fusion.2), channel_id=1, replica_groups=mesh['groups'=2,'cubes'=16] {'cubes'}, dimensions={0}, use_global_device_ids=true | all-gather | bytes 348160 | tf_op jit(solution)/shard_map/all_gather | solution.py:84
  (524 shorter events, 71.6 us)
Async XLA Ops:
  2.6 27.3 %copy-start.4 = (bf16[128,2560]{1,0:T(8,128)(2,1)S(1)}, bf16[128,2560]{1,0:T(8,128)(2,1)}, u32[]{:S(2)}) copy-start(bf16[128,2560]{1,0:T(8,128)(2,1)} %param.9) | copy-start | bytes 1966084
  25.4 4.9 copy-start.2
  32.9 11.3 %copy-start = (bf16[40,64,128]{2,1,0:T(8,128)(2,1)}, bf16[40,64,128]{2,1,0:T(8,128)(2,1)S(1)}, u32[]{:S(2)}) copy-start(bf16[40,64,128]{2,1,0:T(8,128)(2,1)S(1)} %get-tuple-element.292) | copy-start | bytes 1966084 | tf_op jit(solution)/shard_map/while
  33.0 12.7 %copy-start.11 = (s32[11,32]{1,0:T(8,128)}, s32[11,32]{1,0:T(8,128)S(1)}, u32[]{:S(2)}) copy-start(s32[11,32]{1,0:T(8,128)S(1)} %get-tuple-element.291) | copy-start | bytes 4228 | tf_op jit(solution)/shard_map/while
  36.8 30.3 %all-to-all-start = ((bf16[32,64,256]{2,1,0:T(8,128)(2,1)}), bf16[32,64,256]{2,1,0:T(8,128)(2,1)S(1)}, u32[]{:S(2)}, u32[]{:S(2)}) async-start(bf16[32,64,256]{2,1,0:T(8,128)(2,1)} %select_select_fusion.3), calls=%async_computation | async-start | bytes 2097152 | tf_op jit(solution)/shard_map/while/body/eval_jaxpr/all_to_all | solution.py:163
  70.8 1.9 copy-start.1
  72.8 10.7 %copy-start = (bf16[40,64,128]{2,1,0:T(8,128)(2,1)}, bf16[40,64,128]{2,1,0:T(8,128)(2,1)S(1)}, u32[]{:S(2)}) copy-start(bf16[40,64,128]{2,1,0:T(8,128)(2,1)S(1)} %get-tuple-element.292) | copy-start | bytes 1966084 | tf_op jit(solution)/shard_map/while
  72.8 12.1 %copy-start.11 = (s32[11,32]{1,0:T(8,128)}, s32[11,32]{1,0:T(8,128)S(1)}, u32[]{:S(2)}) copy-start(s32[11,32]{1,0:T(8,128)S(1)} %get-tuple-element.291) | copy-start | bytes 4228 | tf_op jit(solution)/shard_map/while
  76.6 29.7 %all-to-all-start = ((bf16[32,64,256]{2,1,0:T(8,128)(2,1)}), bf16[32,64,256]{2,1,0:T(8,128)(2,1)S(1)}, u32[]{:S(2)}, u32[]{:S(2)}) async-start(bf16[32,64,256]{2,1,0:T(8,128)(2,1)} %select_select_fusion.3), calls=%async_computation | async-start | bytes 2097152 | tf_op jit(solution)/shard_map/while/body/eval_jaxpr/all_to_all | solution.py:163
  110.1 1.9 copy-start.1
  110.1 1.9 copy-start.10
  110.1 1.9 copy-start.12
  112.0 10.7 %copy-start = (bf16[40,64,128]{2,1,0:T(8,128)(2,1)}, bf16[40,64,128]{2,1,0:T(8,128)(2,1)S(1)}, u32[]{:S(2)}) copy-start(bf16[40,64,128]{2,1,0:T(8,128)(2,1)S(1)} %get-tuple-element.292) | copy-start | bytes 1966084 | tf_op jit(solution)/shard_map/while
  112.0 12.1 %copy-start.11 = (s32[11,32]{1,0:T(8,128)}, s32[11,32]{1,0:T(8,128)S(1)}, u32[]{:S(2)}) copy-start(s32[11,32]{1,0:T(8,128)S(1)} %get-tuple-element.291) | copy-start | bytes 4228 | tf_op jit(solution)/shard_map/while
  115.8 29.7 %all-to-all-start = ((bf16[32,64,256]{2,1,0:T(8,128)(2,1)}), bf16[32,64,256]{2,1,0:T(8,128)(2,1)S(1)}, u32[]{:S(2)}, u32[]{:S(2)}) async-start(bf16[32,64,256]{2,1,0:T(8,128)(2,1)} %select_select_fusion.3), calls=%async_computation | async-start | bytes 2097152 | tf_op jit(solution)/shard_map/while/body/eval_jaxpr/all_to_all | solution.py:163
  149.3 1.9 copy-start.1
  149.3 1.9 copy-start.10
  149.3 1.9 copy-start.12
  151.2 10.7 %copy-start = (bf16[40,64,128]{2,1,0:T(8,128)(2,1)}, bf16[40,64,128]{2,1,0:T(8,128)(2,1)S(1)}, u32[]{:S(2)}) copy-start(bf16[40,64,128]{2,1,0:T(8,128)(2,1)S(1)} %get-tuple-element.292) | copy-start | bytes 1966084 | tf_op jit(solution)/shard_map/while
  151.2 12.1 %copy-start.11 = (s32[11,32]{1,0:T(8,128)}, s32[11,32]{1,0:T(8,128)S(1)}, u32[]{:S(2)}) copy-start(s32[11,32]{1,0:T(8,128)S(1)} %get-tuple-element.291) | copy-start | bytes 4228 | tf_op jit(solution)/shard_map/while
  155.1 29.7 %all-to-all-start = ((bf16[32,64,256]{2,1,0:T(8,128)(2,1)}), bf16[32,64,256]{2,1,0:T(8,128)(2,1)S(1)}, u32[]{:S(2)}, u32[]{:S(2)}) async-start(bf16[32,64,256]{2,1,0:T(8,128)(2,1)} %select_select_fusion.3), calls=%async_computation | async-start | bytes 2097152 | tf_op jit(solution)/shard_map/while/body/eval_jaxpr/all_to_all | solution.py:163
  188.5 1.9 copy-start.1
  188.5 1.9 copy-start.10
  188.5 1.9 copy-start.12
  190.4 10.7 %copy-start = (bf16[40,64,128]{2,1,0:T(8,128)(2,1)}, bf16[40,64,128]{2,1,0:T(8,128)(2,1)S(1)}, u32[]{:S(2)}) copy-start(bf16[40,64,128]{2,1,0:T(8,128)(2,1)S(1)} %get-tuple-element.292) | copy-start | bytes 1966084 | tf_op jit(solution)/shard_map/while
  190.5 12.1 %copy-start.11 = (s32[11,32]{1,0:T(8,128)}, s32[11,32]{1,0:T(8,128)S(1)}, u32[]{:S(2)}) copy-start(s32[11,32]{1,0:T(8,128)S(1)} %get-tuple-element.291) | copy-start | bytes 4228 | tf_op jit(solution)/shard_map/while
  194.3 29.7 %all-to-all-start = ((bf16[32,64,256]{2,1,0:T(8,128)(2,1)}), bf16[32,64,256]{2,1,0:T(8,128)(2,1)S(1)}, u32[]{:S(2)}, u32[]{:S(2)}) async-start(bf16[32,64,256]{2,1,0:T(8,128)(2,1)} %select_select_fusion.3), calls=%async_computation | async-start | bytes 2097152 | tf_op jit(solution)/shard_map/while/body/eval_jaxpr/all_to_all | solution.py:163
  227.7 1.9 copy-start.1
  227.7 1.9 copy-start.10
  227.8 1.9 copy-start.12
  229.7 10.7 %copy-start = (bf16[40,64,128]{2,1,0:T(8,128)(2,1)}, bf16[40,64,128]{2,1,0:T(8,128)(2,1)S(1)}, u32[]{:S(2)}) copy-start(bf16[40,64,128]{2,1,0:T(8,128)(2,1)S(1)} %get-tuple-element.292) | copy-start | bytes 1966084 | tf_op jit(solution)/shard_map/while
  229.7 12.1 %copy-start.11 = (s32[11,32]{1,0:T(8,128)}, s32[11,32]{1,0:T(8,128)S(1)}, u32[]{:S(2)}) copy-start(s32[11,32]{1,0:T(8,128)S(1)} %get-tuple-element.291) | copy-start | bytes 4228 | tf_op jit(solution)/shard_map/while
  233.5 29.7 %all-to-all-start = ((bf16[32,64,256]{2,1,0:T(8,128)(2,1)}), bf16[32,64,256]{2,1,0:T(8,128)(2,1)S(1)}, u32[]{:S(2)}, u32[]{:S(2)}) async-start(bf16[32,64,256]{2,1,0:T(8,128)(2,1)} %select_select_fusion.3), calls=%async_computation | async-start | bytes 2097152 | tf_op jit(solution)/shard_map/while/body/eval_jaxpr/all_to_all | solution.py:163
  267.0 1.9 copy-start.1
  267.0 1.9 copy-start.10
  267.0 1.9 copy-start.12
  268.9 10.7 %copy-start = (bf16[40,64,128]{2,1,0:T(8,128)(2,1)}, bf16[40,64,128]{2,1,0:T(8,128)(2,1)S(1)}, u32[]{:S(2)}) copy-start(bf16[40,64,128]{2,1,0:T(8,128)(2,1)S(1)} %get-tuple-element.292) | copy-start | bytes 1966084 | tf_op jit(solution)/shard_map/while
  268.9 12.1 %copy-start.11 = (s32[11,32]{1,0:T(8,128)}, s32[11,32]{1,0:T(8,128)S(1)}, u32[]{:S(2)}) copy-start(s32[11,32]{1,0:T(8,128)S(1)} %get-tuple-element.291) | copy-start | bytes 4228 | tf_op jit(solution)/shard_map/while
  272.7 29.7 %all-to-all-start = ((bf16[32,64,256]{2,1,0:T(8,128)(2,1)}), bf16[32,64,256]{2,1,0:T(8,128)(2,1)S(1)}, u32[]{:S(2)}, u32[]{:S(2)}) async-start(bf16[32,64,256]{2,1,0:T(8,128)(2,1)} %select_select_fusion.3), calls=%async_computation | async-start | bytes 2097152 | tf_op jit(solution)/shard_map/while/body/eval_jaxpr/all_to_all | solution.py:163
  306.2 1.9 copy-start.1
  306.2 1.9 copy-start.10
  306.2 1.9 copy-start.12
  308.1 10.7 %copy-start = (bf16[40,64,128]{2,1,0:T(8,128)(2,1)}, bf16[40,64,128]{2,1,0:T(8,128)(2,1)S(1)}, u32[]{:S(2)}) copy-start(bf16[40,64,128]{2,1,0:T(8,128)(2,1)S(1)} %get-tuple-element.292) | copy-start | bytes 1966084 | tf_op jit(solution)/shard_map/while
  308.1 12.1 %copy-start.11 = (s32[11,32]{1,0:T(8,128)}, s32[11,32]{1,0:T(8,128)S(1)}, u32[]{:S(2)}) copy-start(s32[11,32]{1,0:T(8,128)S(1)} %get-tuple-element.291) | copy-start | bytes 4228 | tf_op jit(solution)/shard_map/while
  312.0 29.7 %all-to-all-start = ((bf16[32,64,256]{2,1,0:T(8,128)(2,1)}), bf16[32,64,256]{2,1,0:T(8,128)(2,1)S(1)}, u32[]{:S(2)}, u32[]{:S(2)}) async-start(bf16[32,64,256]{2,1,0:T(8,128)(2,1)} %select_select_fusion.3), calls=%async_computation | async-start | bytes 2097152 | tf_op jit(solution)/shard_map/while/body/eval_jaxpr/all_to_all | solution.py:163
  345.4 1.9 copy-start.1
  345.4 1.9 copy-start.10
  345.4 1.9 copy-start.12
  347.3 10.7 %copy-start = (bf16[40,64,128]{2,1,0:T(8,128)(2,1)}, bf16[40,64,128]{2,1,0:T(8,128)(2,1)S(1)}, u32[]{:S(2)}) copy-start(bf16[40,64,128]{2,1,0:T(8,128)(2,1)S(1)} %get-tuple-element.292) | copy-start | bytes 1966084 | tf_op jit(solution)/shard_map/while
  347.4 12.1 %copy-start.11 = (s32[11,32]{1,0:T(8,128)}, s32[11,32]{1,0:T(8,128)S(1)}, u32[]{:S(2)}) copy-start(s32[11,32]{1,0:T(8,128)S(1)} %get-tuple-element.291) | copy-start | bytes 4228 | tf_op jit(solution)/shard_map/while
  351.2 29.7 %all-to-all-start = ((bf16[32,64,256]{2,1,0:T(8,128)(2,1)}), bf16[32,64,256]{2,1,0:T(8,128)(2,1)S(1)}, u32[]{:S(2)}, u32[]{:S(2)}) async-start(bf16[32,64,256]{2,1,0:T(8,128)(2,1)} %select_select_fusion.3), calls=%async_computation | async-start | bytes 2097152 | tf_op jit(solution)/shard_map/while/body/eval_jaxpr/all_to_all | solution.py:163
  386.6 10.7 %copy-start = (bf16[40,64,128]{2,1,0:T(8,128)(2,1)}, bf16[40,64,128]{2,1,0:T(8,128)(2,1)S(1)}, u32[]{:S(2)}) copy-start(bf16[40,64,128]{2,1,0:T(8,128)(2,1)S(1)} %get-tuple-element.292) | copy-start | bytes 1966084 | tf_op jit(solution)/shard_map/while
  386.6 12.1 %copy-start.11 = (s32[11,32]{1,0:T(8,128)}, s32[11,32]{1,0:T(8,128)S(1)}, u32[]{:S(2)}) copy-start(s32[11,32]{1,0:T(8,128)S(1)} %get-tuple-element.291) | copy-start | bytes 4228 | tf_op jit(solution)/shard_map/while
  390.4 29.7 %all-to-all-start = ((bf16[32,64,256]{2,1,0:T(8,128)(2,1)}), bf16[32,64,256]{2,1,0:T(8,128)(2,1)S(1)}, u32[]{:S(2)}, u32[]{:S(2)}) async-start(bf16[32,64,256]{2,1,0:T(8,128)(2,1)} %select_select_fusion.3), calls=%async_computation | async-start | bytes 2097152 | tf_op jit(solution)/shard_map/while/body/eval_jaxpr/all_to_all | solution.py:163
  423.9 1.9 copy-start.1
  423.9 1.9 copy-start.10
  423.9 1.9 copy-start.12
  425.8 10.7 %copy-start = (bf16[40,64,128]{2,1,0:T(8,128)(2,1)}, bf16[40,64,128]{2,1,0:T(8,128)(2,1)S(1)}, u32[]{:S(2)}) copy-start(bf16[40,64,128]{2,1,0:T(8,128)(2,1)S(1)} %get-tuple-element.292) | copy-start | bytes 1966084 | tf_op jit(solution)/shard_map/while
  425.8 12.1 %copy-start.11 = (s32[11,32]{1,0:T(8,128)}, s32[11,32]{1,0:T(8,128)S(1)}, u32[]{:S(2)}) copy-start(s32[11,32]{1,0:T(8,128)S(1)} %get-tuple-element.291) | copy-start | bytes 4228 | tf_op jit(solution)/shard_map/while
  429.6 29.7 %all-to-all-start = ((bf16[32,64,256]{2,1,0:T(8,128)(2,1)}), bf16[32,64,256]{2,1,0:T(8,128)(2,1)S(1)}, u32[]{:S(2)}, u32[]{:S(2)}) async-start(bf16[32,64,256]{2,1,0:T(8,128)(2,1)} %select_select_fusion.3), calls=%async_computation | async-start | bytes 2097152 | tf_op jit(solution)/shard_map/while/body/eval_jaxpr/all_to_all | solution.py:163
  463.1 1.9 copy-start.1
  463.1 1.9 copy-start.10
  463.1 1.9 copy-start.12
  467.1 23.8 %copy-start.7 = (bf16[128,2560]{1,0:T(8,128)(2,1)S(1)}, bf16[128,2560]{1,0:T(8,128)(2,1)}, u32[]{:S(2)}) copy-start(bf16[128,2560]{1,0:T(8,128)(2,1)} %param.8) | copy-start | bytes 1966084
  (21 other events, 22.5 us)
